TPU v7x, 512 devices: a whole 4x8x8 slice. The times are simulated.
512 devices in a mesh: chan: 8 (over z), sx: 8 (over x, core), sy: 8 (over y).
Axes of the slice: x: 4, y: 8, z: 8, core: 2. Of those that a mesh axis runs over, the one named last changes fastest.
Arguments:
- volume: bfloat16 [8, 64, 64, 256], P('sx', 'sy', None, 'chan'), may hold values from -6 to 6
- kernel: bfloat16 [27, 256, 256], P(None, 'chan'), may hold values from -0.078125 to 0.078125
- grad_out: bfloat16 [8, 64, 64, 256], P('sx', 'sy', None, 'chan'), may hold values from -6 to 6
Outputs:
- out: bfloat16 [8, 64, 64, 256], P('sx', 'sy', None, 'chan')
- grad_input: bfloat16 [8, 64, 64, 256], P('sx', 'sy', None, 'chan')
- grad_kernel: float32 [27, 256, 256], P(None, 'chan')
All inputs are finite; a program needn't handle non-finite values.
Results may differ from a plain program's by a relative error of at most 0.0015.
Values may be sent and summed in bfloat16 or wider, within the bound.
No kernel may reach another device: no remote copies, remote signals or barrier semaphores. Data moves between devices by JAX's collectives and lax.ppermute only.
A program may use at most 64 MiB of HBM per device.

v0:
```python
import math
import jax
import jax.numpy as jnp
from jax import lax
from jax.sharding import PartitionSpec as P


def padded_2(shard, sides, width):
    for axis, dim in sides:
        count, length = (lax.axis_size(axis), shard.shape[dim])
        up = [(i, (i + 1) % count) for i in range(count - 1)]
        down = [(j, i) for i, j in up]
        last = lax.slice_in_dim(shard, length - width, length, axis=dim)
        leading = lax.slice_in_dim(shard, 0, width, axis=dim)
        before = lax.ppermute(last, axis, up)
        after = lax.ppermute(leading, axis, down)
        shard = jnp.concatenate([before, shard, after], axis=dim)
    return shard


def body(volume, kernel, grad_out):
    size_x, size_y, size_z, own_in = volume.shape
    total_out = kernel.shape[2]
    cells = size_x * size_y * size_z
    rim = padded_2(volume, (("sx", 0), ("sy", 1)), 1)
    padded = jnp.pad(rim, ((0, 0), (0, 0), (1, 1), (0, 0)))
    offsets = [(index // 9, index // 3 % 3, index % 3) for index in range(27)]
    partial_out = jnp.zeros((cells, total_out), jnp.float32)
    for index in range(27):
        a, b, e = offsets[index]
        window = padded[a : a + size_x, b : b + size_y, e : e + size_z].reshape(cells, own_in)
        partial_out = partial_out + jnp.dot(
            window, kernel[index], preferred_element_type=jnp.float32
        )
    partial_out = partial_out.reshape(size_x, size_y, size_z, total_out)
    out = lax.psum_scatter(partial_out, "chan", scatter_dimension=3, tiled=True).astype(
        jnp.bfloat16
    )
    grad_full = lax.all_gather(grad_out, "chan", axis=3, tiled=True)
    grad_rimmed = padded_2(grad_full, (("sx", 0), ("sy", 1)), 1)
    grad_padded = jnp.pad(grad_rimmed, ((0, 0), (0, 0), (1, 1), (0, 0)))
    flat_grad = grad_full.reshape(cells, total_out)
    back = jnp.zeros((cells, own_in), jnp.float32)
    kernel_terms = []
    for index in range(27):
        a, b, e = offsets[index]
        window = grad_padded[
            2 - a : 2 - a + size_x, 2 - b : 2 - b + size_y, 2 - e : 2 - e + size_z
        ].reshape(cells, total_out)
        back = back + lax.dot_general(
            window, kernel[index], (((1,), (1,)), ((), ())), preferred_element_type=jnp.float32
        )
        in_window = padded[a : a + size_x, b : b + size_y, e : e + size_z].reshape(cells, own_in)
        kernel_terms.append(
            lax.dot_general(
                in_window, flat_grad, (((0,), (0,)), ((), ())), preferred_element_type=jnp.float32
            )
        )
    grad_input = back.reshape(size_x, size_y, size_z, own_in).astype(jnp.bfloat16)
    local_kernel = jnp.stack(kernel_terms)
    summed = lax.psum(local_kernel, ("sx", "sy"))
    all_cells = cells * lax.axis_size("sx") * lax.axis_size("sy")
    grad_kernel = summed / jnp.float32(math.sqrt(all_cells))
    return (out, grad_input, grad_kernel)


def solution(mesh):
    return jax.shard_map(
        body,
        mesh=mesh,
        in_specs=(P("sx", "sy", None, "chan"), P(None, "chan", None), P("sx", "sy", None, "chan")),
        out_specs=(P("sx", "sy", None, "chan"), P("sx", "sy", None, "chan"), P(None, "chan", None)),
        check_vma=False,
    )
```

profile of v0, /device:TPU:25, one launch (start us, length us, event | category | flops | bytes accessed | tf_op | source)
XLA Modules:
  0.0 342.9 jit_solution(3898932481704692713)
XLA Ops:
  8.1 3.7 %collective-permute-start = (bf16[1,8,64,32]{2,3,1,0:T(8,128)(2,1)}, bf16[1,8,64,32]{2,3,1,0:T(8,128)(2,1)S(1)}, u32[]{:S(2)}, u32[]{:S(2)}) collective-permute-start(bf16[1,8,64,32]{2,3,1,0:T(8,128)(2,1)} %param.3), channel_id=1, source_target_pairs={{0,8},{8,16},{16,24},{24,32},{32,40},{40,48},{48,56},{1,9},{9,17},... | collective-permute-start | bytes 98312 | tf_op jit(solution)/shard_map/ppermute | solution.py:15
  11.7 1.9 collective-permute-start.1
  15.5 2.1 collective-permute-done.1
  17.6 2.1 collective-permute-start.3
  19.7 4.4 %collective-permute-start.2 = (bf16[3,1,64,32]{2,3,1,0:T(8,128)(2,1)S(1)}, bf16[3,1,64,32]{2,3,1,0:T(8,128)(2,1)S(1)}, u32[]{:S(2)}, u32[]{:S(2)}) collective-permute-start(bf16[3,1,64,32]{2,3,1,0:T(8,128)(2,1)S(1)} %get-tuple-element.68), channel_id=1, source_target_pairs={{0,1},{1,2},{2,3},{3,4},{4,5},{5,6},{6,7},{8,9},{9,10},{10,11},{11... | collective-permute-start | bytes 36872 | tf_op jit(solution)/shard_map/ppermute | solution.py:15
  24.1 26.2 %all_gather.3 = bf16[1,8,64,256]{2,1,0,3:T(8,128)(2,1)S(1)} all-gather(bf16[1,8,64,32]{2,1,0,3:T(8,128)(2,1)S(1)} %copy.98), channel_id=1, replica_groups=mesh['chan'=8,'sx'=8,'sy'=8] {'chan'}, dimensions={3}, use_global_device_ids=true | all-gather | bytes 294912 | tf_op jit(solution)/shard_map/all_gather | solution.py:39
  50.6 5.5 %collective-permute-start.5 = (bf16[1,8,64,256]{3,2,1,0:T(8,128)(2,1)S(1)}, bf16[1,8,64,256]{3,2,1,0:T(8,128)(2,1)S(1)}, u32[]{:S(2)}, u32[]{:S(2)}) collective-permute-start(bf16[1,8,64,256]{3,2,1,0:T(8,128)(2,1)S(1)} %copy.99), channel_id=1, source_target_pairs={{8,0},{16,8},{24,16},{32,24},{40,32},{48,40},{56,48},{9,1},{17,9},... | collective-permute-start | bytes 786440 | tf_op jit(solution)/shard_map/ppermute | solution.py:16
  56.1 4.7 %collective-permute-start.4 = (bf16[1,8,64,256]{3,2,1,0:T(8,128)(2,1)S(1)}, bf16[1,8,64,256]{3,2,1,0:T(8,128)(2,1)S(1)}, u32[]{:S(2)}, u32[]{:S(2)}) collective-permute-start(bf16[1,8,64,256]{3,2,1,0:T(8,128)(2,1)S(1)} %copy.99), channel_id=1, source_target_pairs={{0,8},{8,16},{16,24},{24,32},{32,40},{40,48},{48,56},{1,9},{9,17},... | collective-permute-start | bytes 786440 | tf_op jit(solution)/shard_map/ppermute | solution.py:15
  74.5 1.6 reshape.329
  77.6 1.6 reshape.330
  83.7 1.6 reshape.332
  88.1 1.6 reshape.334
  90.3 1.6 reshape.335
  93.4 1.6 reshape.337
  96.4 1.6 reshape.338
  100.9 1.6 reshape.340
  103.9 1.6 reshape.341
  109.2 1.6 reshape.343
  112.2 1.6 reshape.344
  114.5 1.6 reshape.347
  146.8 1.9 collective-permute-start.7
  148.7 4.8 %collective-permute-start.6 = (bf16[3,1,64,256]{3,2,1,0:T(8,128)(2,1)S(1)}, bf16[3,1,64,256]{3,2,1,0:T(8,128)(2,1)S(1)}, u32[]{:S(2)}, u32[]{:S(2)}) collective-permute-start(bf16[3,1,64,256]{3,2,1,0:T(8,128)(2,1)S(1)} %get-tuple-element.39), channel_id=1, source_target_pairs={{0,1},{1,2},{2,3},{3,4},{4,5},{5,6},{6,7},{8,9},{9,10},{10,11},{11... | collective-permute-start | bytes 294920 | tf_op jit(solution)/shard_map/ppermute | solution.py:15
  162.8 168.9 %all-reduce.4.cloned.1.call-done = f32[27,32,256]{2,1,0:T(8,128)} async-done(((f32[27,32,256]{2,1,0:T(8,128)}), f32[27,32,256]{2,1,0:T(8,128)}) %all-reduce.4.cloned.1.call-update) | async-done | bytes 884752 | tf_op jit(solution)/shard_map/psum | solution.py:61
  331.7 2.2 broadcast_multiply_fusion
  (229 shorter events, 79.6 us)
Async XLA Ops:
  8.0 52.8 %copy-start.4 = (bf16[1,8,64,32]{2,3,1,0:T(8,128)(2,1)S(1)}, bf16[1,8,64,32]{2,3,1,0:T(8,128)(2,1)}, u32[]{:S(2)}) copy-start(bf16[1,8,64,32]{2,3,1,0:T(8,128)(2,1)} %param.3) | copy-start | bytes 98308
  8.0 323.7 %all-reduce.4.cloned.1.call-start = ((), (), s32[]{:S(2)}) async-start(), calls=%async_computation.2 | async-start | bytes 1769472 | tf_op jit(solution)/shard_map/psum | solution.py:61
  8.1 6.5 %collective-permute-start = (bf16[1,8,64,32]{2,3,1,0:T(8,128)(2,1)}, bf16[1,8,64,32]{2,3,1,0:T(8,128)(2,1)S(1)}, u32[]{:S(2)}, u32[]{:S(2)}) collective-permute-start(bf16[1,8,64,32]{2,3,1,0:T(8,128)(2,1)} %param.3), channel_id=1, source_target_pairs={{0,8},{8,16},{16,24},{24,32},{32,40},{40,48},{48,56},{1,9},{9,17},... | collective-permute-start | bytes 98312 | tf_op jit(solution)/shard_map/ppermute | solution.py:15
  11.7 5.8 %collective-permute-start.1 = (bf16[1,8,64,32]{2,3,1,0:T(8,128)(2,1)}, bf16[1,8,64,32]{2,3,1,0:T(8,128)(2,1)S(1)}, u32[]{:S(2)}, u32[]{:S(2)}) collective-permute-start(bf16[1,8,64,32]{2,3,1,0:T(8,128)(2,1)} %param.3), channel_id=1, source_target_pairs={{8,0},{16,8},{24,16},{32,24},{40,32},{48,40},{56,48},{9,1},{17,9},... | collective-permute-start | bytes 98312 | tf_op jit(solution)/shard_map/ppermute | solution.py:16
  14.6 47.1 %copy-start.8 = (bf16[1,8,64,32]{2,3,1,0:T(8,128)(2,1)}, bf16[1,8,64,32]{2,3,1,0:T(8,128)(2,1)S(1)}, u32[]{:S(2)}) copy-start(bf16[1,8,64,32]{2,3,1,0:T(8,128)(2,1)S(1)} %collective-permute-done) | copy-start | bytes 98308
  17.5 45.0 %copy-start.6 = (bf16[1,8,64,32]{2,3,1,0:T(8,128)(2,1)}, bf16[1,8,64,32]{2,3,1,0:T(8,128)(2,1)S(1)}, u32[]{:S(2)}) copy-start(bf16[1,8,64,32]{2,3,1,0:T(8,128)(2,1)S(1)} %collective-permute-done.1) | copy-start | bytes 98308
  17.6 44.9 %collective-permute-start.3 = (bf16[3,1,64,32]{2,3,1,0:T(8,128)(2,1)S(1)}, bf16[3,1,64,32]{2,3,1,0:T(8,128)(2,1)S(1)}, u32[]{:S(2)}, u32[]{:S(2)}) collective-permute-start(bf16[3,1,64,32]{2,3,1,0:T(8,128)(2,1)S(1)} %get-tuple-element.69), channel_id=1, source_target_pairs={{1,0},{2,1},{3,2},{4,3},{5,4},{6,5},{7,6},{9,8},{10,9},{11,10},{12... | collective-permute-start | bytes 36872 | tf_op jit(solution)/shard_map/ppermute | solution.py:16
  19.7 42.9 %collective-permute-start.2 = (bf16[3,1,64,32]{2,3,1,0:T(8,128)(2,1)S(1)}, bf16[3,1,64,32]{2,3,1,0:T(8,128)(2,1)S(1)}, u32[]{:S(2)}, u32[]{:S(2)}) collective-permute-start(bf16[3,1,64,32]{2,3,1,0:T(8,128)(2,1)S(1)} %get-tuple-element.68), channel_id=1, source_target_pairs={{0,1},{1,2},{2,3},{3,4},{4,5},{5,6},{6,7},{8,9},{9,10},{10,11},{11... | collective-permute-start | bytes 36872 | tf_op jit(solution)/shard_map/ppermute | solution.py:15
  50.6 96.1 %collective-permute-start.5 = (bf16[1,8,64,256]{3,2,1,0:T(8,128)(2,1)S(1)}, bf16[1,8,64,256]{3,2,1,0:T(8,128)(2,1)S(1)}, u32[]{:S(2)}, u32[]{:S(2)}) collective-permute-start(bf16[1,8,64,256]{3,2,1,0:T(8,128)(2,1)S(1)} %copy.99), channel_id=1, source_target_pairs={{8,0},{16,8},{24,16},{32,24},{40,32},{48,40},{56,48},{9,1},{17,9},... | collective-permute-start | bytes 786440 | tf_op jit(solution)/shard_map/ppermute | solution.py:16
  56.1 90.7 %collective-permute-start.4 = (bf16[1,8,64,256]{3,2,1,0:T(8,128)(2,1)S(1)}, bf16[1,8,64,256]{3,2,1,0:T(8,128)(2,1)S(1)}, u32[]{:S(2)}, u32[]{:S(2)}) collective-permute-start(bf16[1,8,64,256]{3,2,1,0:T(8,128)(2,1)S(1)} %copy.99), channel_id=1, source_target_pairs={{0,8},{8,16},{16,24},{24,32},{32,40},{40,48},{48,56},{1,9},{9,17},... | collective-permute-start | bytes 786440 | tf_op jit(solution)/shard_map/ppermute | solution.py:15
  63.9 2.3 copy-start
  68.5 18.9 %copy-start.14 = (bf16[1,8,64,32]{2,3,1,0:T(8,128)(2,1)S(1)}, bf16[1,8,64,32]{2,3,1,0:T(8,128)(2,1)}, u32[]{:S(2)}) copy-start(bf16[1,8,64,32]{2,3,1,0:T(8,128)(2,1)} %get-tuple-element.51) | copy-start | bytes 98308
  68.5 21.2 %copy-start.13 = (bf16[1,8,64,32]{2,3,1,0:T(8,128)(2,1)S(1)}, bf16[1,8,64,32]{2,3,1,0:T(8,128)(2,1)}, u32[]{:S(2)}) copy-start(bf16[1,8,64,32]{2,3,1,0:T(8,128)(2,1)} %get-tuple-element.50) | copy-start | bytes 98308
  74.5 25.7 %copy-start.12 = (bf16[1,8,64,32]{2,3,1,0:T(8,128)(2,1)S(1)}, bf16[1,8,64,32]{2,3,1,0:T(8,128)(2,1)}, u32[]{:S(2)}) copy-start(bf16[1,8,64,32]{2,3,1,0:T(8,128)(2,1)} %get-tuple-element.47) | copy-start | bytes 98308
  88.1 25.7 %copy-start.11 = (bf16[1,8,64,32]{2,3,1,0:T(8,128)(2,1)S(1)}, bf16[1,8,64,32]{2,3,1,0:T(8,128)(2,1)}, u32[]{:S(2)}) copy-start(bf16[1,8,64,32]{2,3,1,0:T(8,128)(2,1)} %get-tuple-element.42) | copy-start | bytes 98308
  90.3 25.7 %copy-start.3 = (bf16[1,8,64,32]{2,3,1,0:T(8,128)(2,1)S(1)}, bf16[1,8,64,32]{2,3,1,0:T(8,128)(2,1)}, u32[]{:S(2)}) copy-start(bf16[1,8,64,32]{2,3,1,0:T(8,128)(2,1)} %copy-done.2) | copy-start | bytes 98308
  102.4 16.1 %copy-start.9 = (bf16[1,8,64,32]{2,3,1,0:T(8,128)(2,1)S(1)}, bf16[1,8,64,32]{2,3,1,0:T(8,128)(2,1)}, u32[]{:S(2)}) copy-start(bf16[1,8,64,32]{2,3,1,0:T(8,128)(2,1)} %copy-done.8) | copy-start | bytes 98308
  116.0 5.0 %copy-start.1 = (bf16[1,8,64,32]{2,3,1,0:T(8,128)(2,1)S(1)}, bf16[1,8,64,32]{2,3,1,0:T(8,128)(2,1)}, u32[]{:S(2)}) copy-start(bf16[1,8,64,32]{2,3,1,0:T(8,128)(2,1)} %get-tuple-element.60) | copy-start | bytes 98308
  121.0 5.0 %copy-start.5 = (bf16[1,8,64,32]{2,3,1,0:T(8,128)(2,1)S(1)}, bf16[1,8,64,32]{2,3,1,0:T(8,128)(2,1)}, u32[]{:S(2)}) copy-start(bf16[1,8,64,32]{2,3,1,0:T(8,128)(2,1)} %param.3) | copy-start | bytes 98308
  128.6 5.0 %copy-start.7 = (bf16[1,8,64,32]{2,3,1,0:T(8,128)(2,1)S(1)}, bf16[1,8,64,32]{2,3,1,0:T(8,128)(2,1)}, u32[]{:S(2)}) copy-start(bf16[1,8,64,32]{2,3,1,0:T(8,128)(2,1)} %copy-done.6) | copy-start | bytes 98308
  134.4 3.5 %copy-start.17 = (bf16[512,32]{0,1:T(8,128)(2,1)S(1)}, bf16[512,32]{0,1:T(8,128)(2,1)}, u32[]{:S(2)}) copy-start(bf16[512,32]{0,1:T(8,128)(2,1)} %reshape.324) | copy-start | bytes 98308
  137.8 196.1 %reduce-scatter.2.cloned.1.call-start = ((), (), s32[]{:S(2)}) async-start(), calls=%async_computation.1 | async-start | bytes 1179648 | tf_op jit(solution)/shard_map/reduce_scatter | solution.py:36
  146.8 8.3 %collective-permute-start.7 = (bf16[3,1,64,256]{3,2,1,0:T(8,128)(2,1)S(1)}, bf16[3,1,64,256]{3,2,1,0:T(8,128)(2,1)S(1)}, u32[]{:S(2)}, u32[]{:S(2)}) collective-permute-start(bf16[3,1,64,256]{3,2,1,0:T(8,128)(2,1)S(1)} %get-tuple-element.40), channel_id=1, source_target_pairs={{1,0},{2,1},{3,2},{4,3},{5,4},{6,5},{7,6},{9,8},{10,9},{11,10},{12... | collective-permute-start | bytes 294920 | tf_op jit(solution)/shard_map/ppermute | solution.py:16
  148.7 6.4 %collective-permute-start.6 = (bf16[3,1,64,256]{3,2,1,0:T(8,128)(2,1)S(1)}, bf16[3,1,64,256]{3,2,1,0:T(8,128)(2,1)S(1)}, u32[]{:S(2)}, u32[]{:S(2)}) collective-permute-start(bf16[3,1,64,256]{3,2,1,0:T(8,128)(2,1)S(1)} %get-tuple-element.39), channel_id=1, source_target_pairs={{0,1},{1,2},{2,3},{3,4},{4,5},{5,6},{6,7},{8,9},{9,10},{10,11},{11... | collective-permute-start | bytes 294920 | tf_op jit(solution)/shard_map/ppermute | solution.py:15
  (24 other events, 18.4 us)
Sparse Core Ops, SparseCore 0:
  137.9 193.7 all-reduce.3
Sparse Core Ops, SparseCore 1:
  155.2 32.7 reduce-scatter.1
where the time goes:
time: 345 us; the launch traced here: 343 us
  waiting for transfers between devices  171 us (50%)
  local copies, waits for them, and re-layouts  60 us (17%)
  matrix products  34.2 us (10%)
  starting transfers between devices  29 us (8%)
  blocking collectives  26.2 us (8%)
  between operations  16.2 us (5%)
  other arithmetic  6.23 us (2%)
    psum x1, waiting for transfers between devices, body(): summed = lax.psum(local_kernel, ('sx', 'sy'))  169 us
    reshape x27, local copies, waits for them, and re-layouts, body(): padded[a:a + size_x, b:b + size_y, e:e + size_z].reshape(cells, own_in)  29.3 us
    all_gather x1, blocking collectives, body(): grad_full = lax.all_gather(grad_out, 'chan', axis=3, tiled=True)  26.2 us
    dot_general x27, matrix products, body(): lax.dot_general(in_window, flat_grad, (((0,), (0,)), ((), ())), preferred...  22.6 us
    slice x25, local copies, waits for them, and re-layouts, body(): padded[a:a + size_x, b:b + size_y, e:e + size_z].reshape(cells, own_in)  21 us
    ppermute x4, starting transfers between devices, padded_2(): before = lax.ppermute(last, axis, up)  17.6 us
    ppermute x4, starting transfers between devices, padded_2(): after = lax.ppermute(leading, axis, down)  11.4 us
    unnamed x81, local copies, waits for them, and re-layouts  6.98 us
  transfers between devices with their start and end apart: 10, of which 2 were waited for; matrix products, arithmetic and copies ran while one was open for 28% of the time, Pallas kernels for 0%

commit v1 on v0

--- a/solution.py
+++ b/solution.py
@@ -58,7 +58,7 @@
         )
     grad_input = back.reshape(size_x, size_y, size_z, own_in).astype(jnp.bfloat16)
     local_kernel = jnp.stack(kernel_terms)
-    summed = lax.psum(local_kernel, ("sx", "sy"))
+    summed = lax.psum(lax.psum(local_kernel, "sx"), "sy")
     all_cells = cells * lax.axis_size("sx") * lax.axis_size("sy")
     grad_kernel = summed / jnp.float32(math.sqrt(all_cells))
     return (out, grad_input, grad_kernel)

time: 345 us -> 301 us (0.87)
  the two profiles are of different devices: /device:TPU:25 before, /device:TPU:2 now
where the time goes in v1:
time: 301 us; the launch traced here: 299 us
  waiting for transfers between devices  128 us (43%)
  local copies, waits for them, and re-layouts  60 us (20%)
  matrix products  34.2 us (11%)
  blocking collectives  31.9 us (11%)
  starting transfers between devices  21.9 us (7%)
  between operations  16.2 us (5%)
  other arithmetic  6.23 us (2%)
    psum x2, waiting for transfers between devices, body(): summed = lax.psum(lax.psum(local_kernel, 'sx'), 'sy')  127 us
    all_gather x1, blocking collectives, body(): grad_full = lax.all_gather(grad_out, 'chan', axis=3, tiled=True)  31.9 us
    reshape x27, local copies, waits for them, and re-layouts, body(): padded[a:a + size_x, b:b + size_y, e:e + size_z].reshape(cells, own_in)  29.3 us
    dot_general x27, matrix products, body(): lax.dot_general(in_window, flat_grad, (((0,), (0,)), ((), ())), preferred...  22.6 us
    slice x25, local copies, waits for them, and re-layouts, body(): padded[a:a + size_x, b:b + size_y, e:e + size_z].reshape(cells, own_in)  21 us
    ppermute x4, starting transfers between devices, padded_2(): before = lax.ppermute(last, axis, up)  13.4 us
    ppermute x4, starting transfers between devices, padded_2(): after = lax.ppermute(leading, axis, down)  8.15 us
    unnamed x81, local copies, waits for them, and re-layouts  6.98 us
  transfers between devices with their start and end apart: 11, of which 4 were waited for; matrix products, arithmetic and copies ran while one was open for 31% of the time, Pallas kernels for 0%

profile of v1, /device:TPU:2, one launch (start us, length us, event | category | flops | bytes accessed | tf_op | source)
XLA Modules:
  0.0 298.6 jit_solution(353161045384151062)
XLA Ops:
  8.1 1.9 collective-permute-start
  10.0 3.6 %collective-permute-start.1 = (bf16[1,8,64,32]{2,3,1,0:T(8,128)(2,1)}, bf16[1,8,64,32]{2,3,1,0:T(8,128)(2,1)S(1)}, u32[]{:S(2)}, u32[]{:S(2)}) collective-permute-start(bf16[1,8,64,32]{2,3,1,0:T(8,128)(2,1)} %param.3), channel_id=1, source_target_pairs={{8,0},{16,8},{24,16},{32,24},{40,32},{48,40},{56,48},{9,1},{17,9},... | collective-permute-start | bytes 98312 | tf_op jit(solution)/shard_map/ppermute | solution.py:16
  17.2 4.5 %collective-permute-start.2 = (bf16[3,1,64,32]{2,3,1,0:T(8,128)(2,1)S(1)}, bf16[3,1,64,32]{2,3,1,0:T(8,128)(2,1)S(1)}, u32[]{:S(2)}, u32[]{:S(2)}) collective-permute-start(bf16[3,1,64,32]{2,3,1,0:T(8,128)(2,1)S(1)} %get-tuple-element.68), channel_id=1, source_target_pairs={{0,1},{1,2},{2,3},{3,4},{4,5},{5,6},{6,7},{8,9},{9,10},{10,11},{11... | collective-permute-start | bytes 36872 | tf_op jit(solution)/shard_map/ppermute | solution.py:15
  21.7 31.9 %all_gather.3 = bf16[1,8,64,256]{2,1,0,3:T(8,128)(2,1)S(1)} all-gather(bf16[1,8,64,32]{2,1,0,3:T(8,128)(2,1)S(1)} %copy.98), channel_id=1, replica_groups=mesh['chan'=8,'sx'=8,'sy'=8] {'chan'}, dimensions={3}, use_global_device_ids=true | all-gather | bytes 294912 | tf_op jit(solution)/shard_map/all_gather | solution.py:39
  54.0 1.9 collective-permute-start.5
  55.9 2.4 collective-permute-start.4
  72.0 1.6 reshape.329
  75.1 1.6 reshape.330
  78.2 1.6 reshape.331
  81.2 1.6 reshape.332
  85.6 1.6 reshape.334
  87.8 1.6 reshape.335
  90.9 1.6 reshape.337
  94.0 1.6 reshape.338
  98.4 1.6 reshape.340
  101.4 1.6 reshape.341
  103.6 1.6 reshape.342
  106.7 1.6 reshape.343
  109.7 1.6 reshape.344
  112.0 1.6 reshape.347
  145.6 4.6 %collective-permute-start.6 = (bf16[3,1,64,256]{3,2,1,0:T(8,128)(2,1)S(1)}, bf16[3,1,64,256]{3,2,1,0:T(8,128)(2,1)S(1)}, u32[]{:S(2)}, u32[]{:S(2)}) collective-permute-start(bf16[3,1,64,256]{3,2,1,0:T(8,128)(2,1)S(1)} %get-tuple-element.39), channel_id=1, source_target_pairs={{0,1},{1,2},{2,3},{3,4},{4,5},{5,6},{6,7},{8,9},{9,10},{10,11},{11... | collective-permute-start | bytes 294920 | tf_op jit(solution)/shard_map/ppermute | solution.py:15
  159.1 46.2 %all-reduce.5.cloned.1.call-done = f32[27,32,256]{2,1,0:T(8,128)} async-done(((f32[27,32,256]{2,1,0:T(8,128)}), f32[27,32,256]{2,1,0:T(8,128)}) %all-reduce.5.cloned.1.call-update) | async-done | bytes 884752 | tf_op jit(solution)/shard_map/psum | solution.py:61
  208.4 80.5 %all-reduce.7.cloned.1.call-done = f32[27,32,256]{2,1,0:T(8,128)} async-done(((f32[27,32,256]{2,1,0:T(8,128)}), f32[27,32,256]{2,1,0:T(8,128)}) %all-reduce.7.cloned.1.call-update) | async-done | bytes 884752 | tf_op jit(solution)/shard_map/psum | solution.py:61
  288.9 2.2 broadcast_multiply_fusion
  (232 shorter events, 80.7 us)
Async XLA Ops:
  8.0 50.3 %copy-start.4 = (bf16[1,8,64,32]{2,3,1,0:T(8,128)(2,1)S(1)}, bf16[1,8,64,32]{2,3,1,0:T(8,128)(2,1)}, u32[]{:S(2)}) copy-start(bf16[1,8,64,32]{2,3,1,0:T(8,128)(2,1)} %param.3) | copy-start | bytes 98308
  8.0 197.3 %all-reduce.5.cloned.1.call-start = ((), (), s32[]{:S(2)}) async-start(), calls=%async_computation.2 | async-start | bytes 1769472 | tf_op jit(solution)/shard_map/psum | solution.py:61
  8.1 6.5 %collective-permute-start = (bf16[1,8,64,32]{2,3,1,0:T(8,128)(2,1)}, bf16[1,8,64,32]{2,3,1,0:T(8,128)(2,1)S(1)}, u32[]{:S(2)}, u32[]{:S(2)}) collective-permute-start(bf16[1,8,64,32]{2,3,1,0:T(8,128)(2,1)} %param.3), channel_id=1, source_target_pairs={{0,8},{8,16},{16,24},{24,32},{32,40},{40,48},{48,56},{1,9},{9,17},... | collective-permute-start | bytes 98312 | tf_op jit(solution)/shard_map/ppermute | solution.py:15
  10.0 5.9 %collective-permute-start.1 = (bf16[1,8,64,32]{2,3,1,0:T(8,128)(2,1)}, bf16[1,8,64,32]{2,3,1,0:T(8,128)(2,1)S(1)}, u32[]{:S(2)}, u32[]{:S(2)}) collective-permute-start(bf16[1,8,64,32]{2,3,1,0:T(8,128)(2,1)} %param.3), channel_id=1, source_target_pairs={{8,0},{16,8},{24,16},{32,24},{40,32},{48,40},{56,48},{9,1},{17,9},... | collective-permute-start | bytes 98312 | tf_op jit(solution)/shard_map/ppermute | solution.py:16
  14.5 44.6 %copy-start.8 = (bf16[1,8,64,32]{2,3,1,0:T(8,128)(2,1)}, bf16[1,8,64,32]{2,3,1,0:T(8,128)(2,1)S(1)}, u32[]{:S(2)}) copy-start(bf16[1,8,64,32]{2,3,1,0:T(8,128)(2,1)S(1)} %collective-permute-done) | copy-start | bytes 98308
  15.8 44.2 %copy-start.6 = (bf16[1,8,64,32]{2,3,1,0:T(8,128)(2,1)}, bf16[1,8,64,32]{2,3,1,0:T(8,128)(2,1)S(1)}, u32[]{:S(2)}) copy-start(bf16[1,8,64,32]{2,3,1,0:T(8,128)(2,1)S(1)} %collective-permute-done.1) | copy-start | bytes 98308
  15.9 44.2 %collective-permute-start.3 = (bf16[3,1,64,32]{2,3,1,0:T(8,128)(2,1)S(1)}, bf16[3,1,64,32]{2,3,1,0:T(8,128)(2,1)S(1)}, u32[]{:S(2)}, u32[]{:S(2)}) collective-permute-start(bf16[3,1,64,32]{2,3,1,0:T(8,128)(2,1)S(1)} %get-tuple-element.69), channel_id=1, source_target_pairs={{1,0},{2,1},{3,2},{4,3},{5,4},{6,5},{7,6},{9,8},{10,9},{11,10},{12... | collective-permute-start | bytes 36872 | tf_op jit(solution)/shard_map/ppermute | solution.py:16
  17.2 42.9 %collective-permute-start.2 = (bf16[3,1,64,32]{2,3,1,0:T(8,128)(2,1)S(1)}, bf16[3,1,64,32]{2,3,1,0:T(8,128)(2,1)S(1)}, u32[]{:S(2)}, u32[]{:S(2)}) collective-permute-start(bf16[3,1,64,32]{2,3,1,0:T(8,128)(2,1)S(1)} %get-tuple-element.68), channel_id=1, source_target_pairs={{0,1},{1,2},{2,3},{3,4},{4,5},{5,6},{6,7},{8,9},{9,10},{10,11},{11... | collective-permute-start | bytes 36872 | tf_op jit(solution)/shard_map/ppermute | solution.py:15
  54.0 90.3 %collective-permute-start.5 = (bf16[1,8,64,256]{3,2,1,0:T(8,128)(2,1)S(1)}, bf16[1,8,64,256]{3,2,1,0:T(8,128)(2,1)S(1)}, u32[]{:S(2)}, u32[]{:S(2)}) collective-permute-start(bf16[1,8,64,256]{3,2,1,0:T(8,128)(2,1)S(1)} %copy.99), channel_id=1, source_target_pairs={{8,0},{16,8},{24,16},{32,24},{40,32},{48,40},{56,48},{9,1},{17,9},... | collective-permute-start | bytes 786440 | tf_op jit(solution)/shard_map/ppermute | solution.py:16
  55.9 88.4 %collective-permute-start.4 = (bf16[1,8,64,256]{3,2,1,0:T(8,128)(2,1)S(1)}, bf16[1,8,64,256]{3,2,1,0:T(8,128)(2,1)S(1)}, u32[]{:S(2)}, u32[]{:S(2)}) collective-permute-start(bf16[1,8,64,256]{3,2,1,0:T(8,128)(2,1)S(1)} %copy.99), channel_id=1, source_target_pairs={{0,8},{8,16},{16,24},{24,32},{32,40},{40,48},{48,56},{1,9},{9,17},... | collective-permute-start | bytes 786440 | tf_op jit(solution)/shard_map/ppermute | solution.py:15
  66.0 18.9 %copy-start.14 = (bf16[1,8,64,32]{2,3,1,0:T(8,128)(2,1)S(1)}, bf16[1,8,64,32]{2,3,1,0:T(8,128)(2,1)}, u32[]{:S(2)}) copy-start(bf16[1,8,64,32]{2,3,1,0:T(8,128)(2,1)} %get-tuple-element.51) | copy-start | bytes 98308
  66.0 21.2 %copy-start.13 = (bf16[1,8,64,32]{2,3,1,0:T(8,128)(2,1)S(1)}, bf16[1,8,64,32]{2,3,1,0:T(8,128)(2,1)}, u32[]{:S(2)}) copy-start(bf16[1,8,64,32]{2,3,1,0:T(8,128)(2,1)} %get-tuple-element.50) | copy-start | bytes 98308
  72.0 25.7 %copy-start.12 = (bf16[1,8,64,32]{2,3,1,0:T(8,128)(2,1)S(1)}, bf16[1,8,64,32]{2,3,1,0:T(8,128)(2,1)}, u32[]{:S(2)}) copy-start(bf16[1,8,64,32]{2,3,1,0:T(8,128)(2,1)} %get-tuple-element.47) | copy-start | bytes 98308
  85.6 25.7 %copy-start.11 = (bf16[1,8,64,32]{2,3,1,0:T(8,128)(2,1)S(1)}, bf16[1,8,64,32]{2,3,1,0:T(8,128)(2,1)}, u32[]{:S(2)}) copy-start(bf16[1,8,64,32]{2,3,1,0:T(8,128)(2,1)} %get-tuple-element.42) | copy-start | bytes 98308
  87.8 25.7 %copy-start.3 = (bf16[1,8,64,32]{2,3,1,0:T(8,128)(2,1)S(1)}, bf16[1,8,64,32]{2,3,1,0:T(8,128)(2,1)}, u32[]{:S(2)}) copy-start(bf16[1,8,64,32]{2,3,1,0:T(8,128)(2,1)} %copy-done.2) | copy-start | bytes 98308
  99.9 16.1 %copy-start.9 = (bf16[1,8,64,32]{2,3,1,0:T(8,128)(2,1)S(1)}, bf16[1,8,64,32]{2,3,1,0:T(8,128)(2,1)}, u32[]{:S(2)}) copy-start(bf16[1,8,64,32]{2,3,1,0:T(8,128)(2,1)} %copy-done.8) | copy-start | bytes 98308
  113.5 5.0 %copy-start.1 = (bf16[1,8,64,32]{2,3,1,0:T(8,128)(2,1)S(1)}, bf16[1,8,64,32]{2,3,1,0:T(8,128)(2,1)}, u32[]{:S(2)}) copy-start(bf16[1,8,64,32]{2,3,1,0:T(8,128)(2,1)} %get-tuple-element.60) | copy-start | bytes 98308
  118.6 5.0 %copy-start.5 = (bf16[1,8,64,32]{2,3,1,0:T(8,128)(2,1)S(1)}, bf16[1,8,64,32]{2,3,1,0:T(8,128)(2,1)}, u32[]{:S(2)}) copy-start(bf16[1,8,64,32]{2,3,1,0:T(8,128)(2,1)} %param.3) | copy-start | bytes 98308
  126.1 5.0 %copy-start.7 = (bf16[1,8,64,32]{2,3,1,0:T(8,128)(2,1)S(1)}, bf16[1,8,64,32]{2,3,1,0:T(8,128)(2,1)}, u32[]{:S(2)}) copy-start(bf16[1,8,64,32]{2,3,1,0:T(8,128)(2,1)} %copy-done.6) | copy-start | bytes 98308
  131.9 3.5 %copy-start.17 = (bf16[512,32]{0,1:T(8,128)(2,1)S(1)}, bf16[512,32]{0,1:T(8,128)(2,1)}, u32[]{:S(2)}) copy-start(bf16[512,32]{0,1:T(8,128)(2,1)} %reshape.324) | copy-start | bytes 98308
  135.3 71.5 %reduce-scatter.2.cloned.1.call-start = ((), (), s32[]{:S(2)}) async-start(), calls=%async_computation.1 | async-start | bytes 1179648 | tf_op jit(solution)/shard_map/reduce_scatter | solution.py:36
  144.3 7.7 %collective-permute-start.7 = (bf16[3,1,64,256]{3,2,1,0:T(8,128)(2,1)S(1)}, bf16[3,1,64,256]{3,2,1,0:T(8,128)(2,1)S(1)}, u32[]{:S(2)}, u32[]{:S(2)}) collective-permute-start(bf16[3,1,64,256]{3,2,1,0:T(8,128)(2,1)S(1)} %get-tuple-element.40), channel_id=1, source_target_pairs={{1,0},{2,1},{3,2},{4,3},{5,4},{6,5},{7,6},{9,8},{10,9},{11,10},{12... | collective-permute-start | bytes 294920 | tf_op jit(solution)/shard_map/ppermute | solution.py:16
  145.6 7.4 %collective-permute-start.6 = (bf16[3,1,64,256]{3,2,1,0:T(8,128)(2,1)S(1)}, bf16[3,1,64,256]{3,2,1,0:T(8,128)(2,1)S(1)}, u32[]{:S(2)}, u32[]{:S(2)}) collective-permute-start(bf16[3,1,64,256]{3,2,1,0:T(8,128)(2,1)S(1)} %get-tuple-element.39), channel_id=1, source_target_pairs={{0,1},{1,2},{2,3},{3,4},{4,5},{5,6},{6,7},{8,9},{9,10},{10,11},{11... | collective-permute-start | bytes 294920 | tf_op jit(solution)/shard_map/ppermute | solution.py:15
  151.8 137.1 %all-reduce.7.cloned.1.call-start = ((), (), s32[]{:S(2)}) async-start(), calls=%async_computation.3 | async-start | bytes 1769472 | tf_op jit(solution)/shard_map/psum | solution.py:61
  (25 other events, 20.6 us)
Sparse Core Ops, SparseCore 0:
  135.5 69.7 all-reduce.4
  207.8 81.0 all-reduce.6
Sparse Core Ops, SparseCore 1:
  151.9 40.4 reduce-scatter.1
